TPU v7x, 32 devices: a whole 2x2x4 slice. The times are simulated.
32 devices in a mesh: mem: 2 (over x), gy: 4 (over z), gx: 4 (over y, core).
Axes of the slice: x: 2, y: 2, z: 4, core: 2. Of those that a mesh axis runs over, the one named last changes fastest.
Arguments:
- alpha: float32 [16, 32, 64, 512], P('mem', None, 'gy', 'gx'), may hold values from -4 to 4
- perturb: bfloat16 [16, 4, 32, 64, 512], P('mem', None, None, 'gy', 'gx'), may hold values from -6 to 6
- chi: float32 [4, 32, 64, 512], P(None, None, 'gy', 'gx'), may hold values from -4 to 4
- kappa: float32 [64, 512], P('gy', 'gx'), may hold values from 0.05 to 0.24
- vert_bounds: int32 [2, 32], replicated, may hold values from 0 to 31, as said below
- static_vert: float32 [4, 32, 32], replicated, may hold values from -1 to 1
- fine_owner: int32 [16, 2], P(('gy', 'gx')), may hold values from 0 to 1, each once within a row
- obs_stencil: int32 [32768], P(('mem', 'gy', 'gx')), may hold values from 0 to 959
- obs_weight: float32 [4, 32768], P(None, ('mem', 'gy', 'gx')), may hold values from 0.05 to 0.5
- background: bfloat16 [32768, 128], P(('mem', 'gy', 'gx')), may hold values from -6 to 6
- observed: float32 [8, 32768], P(None, ('mem', 'gy', 'gx')), may hold values from -6 to 6
- inv_var: float32 [8, 32768], P(None, ('mem', 'gy', 'gx')), may hold values from 2 to 32
- jacobian: float32 [8, 128], replicated, may hold values from -0.5 to 0.5
- obs_count: int32 [32], P(('mem', 'gy', 'gx')), may hold values from 256 to 1024, as said below
Outputs:
- grad_alpha: float32 [16, 32, 64, 512], P('mem', None, 'gy', 'gx')
- grad_chi: float32 [4, 32, 64, 512], P(None, None, 'gy', 'gx')
Inputs may be any that keep to these rules, and one draw needn't show every extreme that they name: `vert_bounds`: row 0 holds each level's lowest and row 1 its highest coupled level; level l lies between both inclusive, and each lies 1 to 4 levels from l unless cut at the ends of the column. `obs_count`: observations below this count in a device's block are live; some device has exactly 1024 and some exactly 256.
All inputs are finite; a program needn't handle non-finite values.
Results may differ from a plain program's by a relative error of at most 0.00099.
Values may be sent and summed in bfloat16 or wider, within the bound.
A program may use at most 128 MiB of HBM per device.

v0:
```python
import math
import jax
import jax.numpy as jnp
from jax import lax
from jax.sharding import PartitionSpec as P

NDIFF = 4
ensemble_weight = 0.8
static_weight = 0.6
vertical_scale = 2.0
highest = lax.Precision.HIGHEST


def padded_2(cells, sides, width):
    for axis, dim in sides:
        count = lax.axis_size(axis)
        head = lax.slice_in_dim(cells, 0, width, axis=dim)
        tail = lax.slice_in_dim(cells, cells.shape[dim] - width, cells.shape[dim], axis=dim)
        cells = jnp.concatenate(
            [
                lax.ppermute(tail, axis, [(i, (i + 1) % count) for i in range(count)]),
                cells,
                lax.ppermute(head, axis, [((i + 1) % count, i) for i in range(count)]),
            ],
            axis=dim,
        )
    return cells


def shifted(value, axis, steps):
    count = lax.axis_size(axis)
    pairs = [(source, (source + steps) % count) for source in range(count)]
    return lax.ppermute(value, axis, pairs)


def vertical_matrix(vert_bounds, levels):
    row_level = lax.broadcasted_iota(jnp.int32, (levels, levels), 0)
    col_level = lax.broadcasted_iota(jnp.int32, (levels, levels), 1)
    inside = (col_level >= vert_bounds[0][:, None]) & (col_level <= vert_bounds[1][:, None])
    distance = jnp.abs(row_level - col_level).astype(jnp.float32)
    return jnp.where(inside, jnp.exp(-distance / vertical_scale), jnp.zeros_like(distance))


def deep_pad(values, margin):
    padded = padded_2(values, (("gy", 2), ("gx", 3)), margin)
    row_place = lax.axis_index("gy")
    upper_rows = jnp.flip(padded[:, :, margin : 2 * margin], axis=2)
    lower_rows = jnp.flip(padded[:, :, -2 * margin : -margin], axis=2)
    north_fixed = jnp.concatenate([upper_rows, padded[:, :, margin:]], axis=2)
    padded = jnp.where(row_place == 0, north_fixed, padded)
    south_fixed = jnp.concatenate([padded[:, :, :-margin], lower_rows], axis=2)
    return jnp.where(row_place == lax.axis_size("gy") - 1, south_fixed, padded)


def stencil_of(padded):
    center = padded[:, :, 1:-1, 1:-1]
    return (
        padded[:, :, :-2, 1:-1]
        + padded[:, :, 2:, 1:-1]
        + padded[:, :, 1:-1, :-2]
        + padded[:, :, 1:-1, 2:]
        - 4.0 * center
    )


def sweep_forward(padded, kappa_pad):
    for repeat in range(NDIFF):
        stencil_sum = stencil_of(padded)
        kappa_pad = kappa_pad[:, :, 1:-1, 1:-1]
        padded = padded[:, :, 1:-1, 1:-1] + kappa_pad * stencil_sum
    return padded


def sweep_adjoint(padded, kappa_pad):
    for repeat in range(NDIFF):
        stencil_sum = stencil_of(kappa_pad * padded)
        kappa_pad = kappa_pad[:, :, 1:-1, 1:-1]
        padded = padded[:, :, 1:-1, 1:-1] + stencil_sum
    return padded


def to_cells(values, column_width):
    return jnp.transpose(values.reshape(column_width, values.shape[2], values.shape[3]), (1, 2, 0))


def from_cells(cell_table, variables, levels):
    return jnp.transpose(cell_table, (2, 0, 1)).reshape(
        variables, levels, cell_table.shape[0], cell_table.shape[1]
    )


def extend_east(cell_table, rim_cols):
    rim_part = shifted(cell_table[:, :rim_cols], "gx", -1)
    return jnp.concatenate([cell_table, rim_part], axis=1)


def fold_east(wide_grad, tile_cols, rim_cols):
    from_west = shifted(wide_grad[:, tile_cols:], "gx", 1)
    head_cols = wide_grad[:, :rim_cols] + from_west
    return jnp.concatenate([head_cols, wide_grad[:, rim_cols:tile_cols]], axis=1)


def observe(region, obs_stencil, obs_weight, background, observed, inv_var, jacobian, obs_count):
    row_count, region_cols, column_width = region.shape
    band_size = region_cols - 1
    slot_table = region.reshape(row_count * region_cols, column_width)
    anchor_row = obs_stencil // band_size
    anchor_col = obs_stencil % band_size
    cell_index = [
        (anchor_row + corner // 2) * region_cols + anchor_col + corner % 2 for corner in range(4)
    ]
    increment_obs = jnp.zeros(background.shape, jnp.float32)
    for corner in range(4):
        picked = jnp.take(slot_table, cell_index[corner], axis=0).astype(jnp.float32)
        increment_obs = increment_obs + obs_weight[corner][:, None] * picked
    bent = jnp.tanh(background.astype(jnp.float32) + increment_obs)
    modeled = jnp.einsum("cv,ov->co", jacobian, bent, precision=highest)
    position = lax.broadcasted_iota(jnp.int32, modeled.shape, 1)
    misfit = jnp.where(
        position < obs_count[0], (modeled - observed) * inv_var, jnp.zeros_like(modeled)
    )
    state_grad = (1.0 - bent * bent) * jnp.einsum("co,cv->ov", misfit, jacobian, precision=highest)
    returned = jnp.zeros(slot_table.shape, jnp.float32)
    for corner in range(4):
        returned = returned.at[cell_index[corner]].add(obs_weight[corner][:, None] * state_grad)
    return returned.reshape(row_count, region_cols, column_width)


def body(
    alpha,
    perturb,
    chi,
    kappa,
    vert_bounds,
    static_vert,
    fine_owner,
    obs_stencil,
    obs_weight,
    background,
    observed,
    inv_var,
    jacobian,
    obs_count,
):
    members, levels, tile_rows, tile_cols = alpha.shape
    variables = perturb.shape[1]
    column_width = variables * levels
    member_groups = lax.axis_size("mem")
    band_width = tile_cols // member_groups
    shift_cols = band_width // 2
    rim_cols = shift_cols + 1
    member_group = lax.axis_index("mem")
    owner_row = fine_owner[0]
    band_ids = lax.broadcasted_iota(jnp.int32, (member_groups, member_groups), 1)
    own_band = jnp.sum(
        jnp.where(owner_row == member_group, band_ids[0], jnp.zeros_like(band_ids[0]))
    )
    region_offsets = lax.broadcasted_iota(jnp.int32, (band_width + 1,), 0)
    ens_scale = ensemble_weight / math.sqrt(members * member_groups - 1)
    vertical = vertical_matrix(vert_bounds, levels)
    spread = jnp.einsum("lm,kmyx->klyx", vertical, alpha, precision=highest)
    kappa_pad = deep_pad(kappa[None, None], NDIFF)
    spread = sweep_forward(deep_pad(spread, NDIFF), kappa_pad)
    partial_sum = jnp.sum(perturb.astype(jnp.float32) * spread[:, None], axis=0)
    member_total = lax.psum(partial_sum, "mem")
    static = jnp.einsum("vlm,vmyx->vlyx", static_vert, chi, precision=highest)
    increment = (ens_scale * member_total + static_weight * static).astype(jnp.bfloat16)
    widened = extend_east(to_cells(increment, column_width), rim_cols)
    own_cols = own_band * band_width + shift_cols + region_offsets
    region = jnp.take(widened, own_cols, axis=1)
    region_grad = observe(
        region, obs_stencil, obs_weight, background, observed, inv_var, jacobian, obs_count
    )
    wide_grad = jnp.zeros(widened.shape, jnp.float32).at[:, own_cols].add(region_grad)
    tile_grad = fold_east(wide_grad, tile_cols, rim_cols)
    gradient_cells = lax.psum(tile_grad, "mem")
    gradient = from_cells(gradient_cells, variables, levels)
    grad_chi = chi + static_weight * jnp.einsum(
        "vlm,vlyx->vmyx", static_vert, gradient, precision=highest
    )
    back_spread = ens_scale * jnp.sum(perturb.astype(jnp.float32) * gradient[None], axis=1)
    back_spread = sweep_adjoint(deep_pad(back_spread, NDIFF), kappa_pad)
    grad_alpha = alpha + jnp.einsum("lm,klyx->kmyx", vertical, back_spread, precision=highest)
    return (grad_alpha, grad_chi)


def solution(mesh):
    in_specs = (
        P("mem", None, "gy", "gx"),
        P("mem", None, None, "gy", "gx"),
        P(None, None, "gy", "gx"),
        P("gy", "gx"),
        P(),
        P(),
        P(("gy", "gx"), None),
        P(("mem", "gy", "gx")),
        P(None, ("mem", "gy", "gx")),
        P(("mem", "gy", "gx"), None),
        P(None, ("mem", "gy", "gx")),
        P(None, ("mem", "gy", "gx")),
        P(),
        P(("mem", "gy", "gx")),
    )
    out_specs = (P("mem", None, "gy", "gx"), P(None, None, "gy", "gx"))
    return jax.shard_map(body, mesh=mesh, in_specs=in_specs, out_specs=out_specs, check_vma=False)
```

profile of v0, /device:TPU:0, one launch (start us, length us, event | category | flops | bytes accessed | tf_op | source)
XLA Modules:
  0.0 408.9 jit_solution(9989891320124790640)
XLA Ops:
  8.0 3.1 collective-permute-start.4
  11.0 2.0 collective-permute-start.5
  13.8 3.9 fusion.28
  18.7 3.8 collective-permute-start.1
  23.4 1.7 collective-permute-start.7
  27.2 8.3 %collective-permute-done = f32[8,32,4,128]{3,1,2,0:T(8,128)S(1)} collective-permute-done((f32[8,32,4,128]{3,1,2,0:T(8,128)}, f32[8,32,4,128]{3,1,2,0:T(8,128)S(1)}, u32[]{:S(2)}, u32[]{:S(2)}) %collective-permute-start) | collective-permute-done | bytes 524320 | tf_op jit(solution)/shard_map/ppermute | solution.py:21
  35.5 8.0 %collective-permute-done.1 = f32[8,32,4,128]{3,1,2,0:T(8,128)S(1)} collective-permute-done((f32[8,32,4,128]{3,1,2,0:T(8,128)}, f32[8,32,4,128]{3,1,2,0:T(8,128)S(1)}, u32[]{:S(2)}, u32[]{:S(2)}) %collective-permute-start.1) | collective-permute-done | bytes 524320 | tf_op jit(solution)/shard_map/ppermute | solution.py:23
  43.9 3.7 fusion.88
  47.6 3.4 copy.52
  51.0 3.4 copy.53
  55.4 10.8 %collective-permute-done.2 = f32[8,32,24,4]{1,2,3,0:T(8,128)} collective-permute-done((f32[8,32,24,4]{1,2,3,0:T(8,128)}, f32[8,32,24,4]{1,2,3,0:T(8,128)}, u32[]{:S(2)}, u32[]{:S(2)}) %collective-permute-start.2) | collective-permute-done | bytes 98336 | tf_op jit(solution)/shard_map/ppermute | solution.py:21
  66.2 3.4 copy.54
  69.6 3.4 copy.55
  72.9 5.7 %pad_maximum_fusion = f32[8,32,24,136]{3,1,2,0:T(8,128)S(1)} fusion(f32[8,32,24,4]{3,1,2,0:T(8,128)} %copy.55, f32[8,32,4,128]{3,1,2,0:T(8,128)S(1)} %collective-permute-done.1, f32[8,32,16,128]{3,1,2,0:T(8,128)S(1)} %fusion.28, f32[8,32,4,128]{3,1,2,0:T(8,128)S(1)} %collective-permute-done, f32[8,32,24,4]{3,1,2,0:T(8,128)} %copy.54), kind=kLoop, calls=%fused_computation.14 | loop fusion | flops 3342336 | bytes 6684672 | tf_op jit(solution)/shard_map/concatenate | solution.py:19
  80.1 2.8 slice.361
  82.9 2.3 rev.21
  85.2 2.3 rev.20
  87.5 6.6 %maximum_select_fusion = f32[8,32,24,136]{3,1,2,0:T(8,128)S(1)} fusion(f32[8,32,20,136]{3,1,2,0:T(8,128)} %slice.361, f32[8,32,4,136]{3,1,2,0:T(8,128)} %rev.20, pred[]{:T(512)S(6)} %eq.20, f32[8,32,24,4]{3,1,2,0:T(8,128)} %copy.55, f32[8,32,4,128]{3,1,2,0:T(8,128)S(1)} %collective-permute-done.1, f32[8,32,16,128]{3,1,2,0:T(8,128)S(1)} %fusion.28, ...), kind=kLoop, calls=%fused_computation.15 | loop fusion | flops 5013504 | bytes 10027009 | tf_op jit(solution)/shard_map/jit(_where)/select_n | solution.py:50
  94.1 2.6 copy-done.2
  96.8 2.8 slice.362
  99.6 5.9 %maximum_select_fusion.1 = f32[8,32,24,136]{3,1,2,0:T(8,128)S(1)} fusion(f32[8,32,24,136]{3,1,2,0:T(8,128)} %copy-done.2, f32[8,32,4,136]{3,1,2,0:T(8,128)S(1)} %copy-done.7, f32[8,32,20,136]{3,1,2,0:T(8,128)} %slice.362, pred[]{:T(512)S(6)} %eq.19), kind=kLoop, calls=%fused_computation.16 | loop fusion | flops 1671168 | bytes 10027009 | tf_op jit(solution)/shard_map/jit(_where)/select_n | solution.py:52
  105.5 6.1 %fusion.6 = f32[8,32,22,134]{3,1,2,0:T(8,128)S(1)} fusion(f32[8,32,24,136]{3,1,2,0:T(8,128)S(1)} %maximum_select_fusion.1, f32[22,134]{1,0:T(8,128)S(1)} %slice_bitcast_fusion.2), kind=kLoop, calls=%fused_computation.29 | loop fusion | flops 5282816 | bytes 18124304 | tf_op jit(solution)/shard_map/add | solution.py:70
  111.6 5.7 %fusion.11 = f32[8,32,20,132]{3,1,2,0:T(8,128)S(1)} fusion(f32[8,32,22,134]{3,1,2,0:T(8,128)S(1)} %fusion.6, f32[20,132]{1,0:T(8,128)S(1)} %slice_bitcast_fusion.1), kind=kLoop, calls=%fused_computation.41 | loop fusion | flops 4730880 | bytes 16230720 | tf_op jit(solution)/shard_map/add | solution.py:70
  117.3 5.0 %fusion.16 = f32[8,32,18,130]{3,1,2,0:T(8,128)S(1)} fusion(f32[8,32,20,132]{3,1,2,0:T(8,128)S(1)} %fusion.11, f32[18,130]{1,0:T(8,128)S(1)} %slice_bitcast_fusion), kind=kLoop, calls=%fused_computation.53 | loop fusion | flops 4193280 | bytes 14386320 | tf_op jit(solution)/shard_map/add | solution.py:70
  122.4 2.2 fusion.25
  129.8 38.5 %all-reduce.3.cloned.1.call-done = f32[4,32,16,128]{3,1,2,0:T(8,128)} async-done(((f32[4,32,16,128]{3,1,2,0:T(8,128)}), f32[4,32,16,128]{3,1,2,0:T(8,128)}) %all-reduce.3.cloned.1.call-update) | async-done | bytes 1048592 | tf_op jit(solution)/shard_map/psum | solution.py:165
  168.3 2.5 fusion.36
  173.0 2.4 collective-permute-done.8
  176.5 3.2 gather_fusion.4
  179.7 3.2 gather_fusion.3
  183.0 3.2 gather_fusion.2
  186.2 3.2 gather_fusion.1
  192.4 6.7 %scatter_custom_fusion = f32[1040,128]{1,0:T(8,128)S(1)} fusion(s32[1024]{0:T(1024)S(1)} %get-tuple-element.64, f32[1024,128]{1,0:T(8,128)S(1)} %convolution_multiply_fusion.2, f32[]{:T(128)} %constant.45.clone.1, f32[1024]{0:T(1024)S(1)} %bitcast.96), kind=kCustom, calls=%fused_computation.103 | custom fusion | flops 262144 | bytes 1060868 | tf_op jit(solution)/shard_map/scatter-add | solution.py:125
  199.0 6.7 %scatter_custom_fusion.1 = f32[1040,128]{1,0:T(8,128)S(1)} fusion(f32[1040,128]{1,0:T(8,128)S(1)} %scatter_custom_fusion, s32[1024]{0:T(1024)S(1)} %get-tuple-element.59, f32[1024,128]{1,0:T(8,128)S(1)} %convolution_multiply_fusion.2, f32[1024]{0:T(1024)S(1)} %bitcast.94), kind=kCustom, calls=%fused_computation.101 | custom fusion | flops 262144 | bytes 1060864 | tf_op jit(solution)/shard_map/scatter-add | solution.py:125
  205.7 6.7 %scatter_custom_fusion.2 = f32[1040,128]{1,0:T(8,128)S(1)} fusion(f32[1040,128]{1,0:T(8,128)S(1)} %scatter_custom_fusion.1, s32[1024]{0:T(1024)S(1)} %get-tuple-element.49, f32[1024,128]{1,0:T(8,128)S(1)} %convolution_multiply_fusion.2, f32[1024]{0:T(1024)S(1)} %bitcast.92), kind=kCustom, calls=%fused_computation.99 | custom fusion | flops 262144 | bytes 1060864 | tf_op jit(solution)/shard_map/scatter-add | solution.py:125
  212.5 7.1 %scatter_custom_fusion.3 = f32[1040,128]{1,0:T(8,128)S(1)} fusion(f32[1040,128]{1,0:T(8,128)S(1)} %scatter_custom_fusion.2, s32[1024]{0:T(1024)S(1)} %get-tuple-element.17, f32[1024,128]{1,0:T(8,128)S(1)} %convolution_multiply_fusion.2, f32[1024]{0:T(1024)S(1)} %bitcast.90), kind=kCustom, calls=%fused_computation.97 | custom fusion | flops 262144 | bytes 1060864 | tf_op jit(solution)/shard_map/scatter-add | solution.py:125
  219.8 3.5 scatter_fusion
  224.4 5.0 %collective-permute-done.9 = f32[16,33,128]{2,0,1:T(8,128)S(1)} collective-permute-done((f32[16,33,128]{2,0,1:T(8,128)S(1)}, f32[16,33,128]{2,0,1:T(8,128)S(1)}, u32[]{:S(2)}, u32[]{:S(2)}) %collective-permute-start.9) | collective-permute-done | bytes 270368 | tf_op jit(solution)/shard_map/ppermute | solution.py:33
  231.6 39.5 %all-reduce.5.cloned.1.call-done = f32[4,32,16,128]{3,1,2,0:T(8,128)} async-done(((f32[4,32,16,128]{3,1,2,0:T(8,128)}), f32[4,32,16,128]{3,1,2,0:T(8,128)}) %all-reduce.5.cloned.1.call-update) | async-done | bytes 1048592 | tf_op jit(solution)/shard_map/psum | solution.py:176
  271.1 1.8 copy.65
  272.9 3.4 fusion.1
  277.2 1.5 collective-permute-start.10
  278.7 2.3 collective-permute-start.11
  281.2 12.7 %collective-permute-done.10 = f32[8,32,4,128]{3,1,2,0:T(8,128)S(1)} collective-permute-done((f32[8,32,4,128]{3,1,2,0:T(8,128)S(1)}, f32[8,32,4,128]{3,1,2,0:T(8,128)S(1)}, u32[]{:S(2)}, u32[]{:S(2)}) %collective-permute-start.10) | collective-permute-done | bytes 524320 | tf_op jit(solution)/shard_map/ppermute | solution.py:21
  293.9 9.3 %collective-permute-done.11 = f32[8,32,4,128]{3,1,2,0:T(8,128)S(1)} collective-permute-done((f32[8,32,4,128]{3,1,2,0:T(8,128)S(1)}, f32[8,32,4,128]{3,1,2,0:T(8,128)S(1)}, u32[]{:S(2)}, u32[]{:S(2)}) %collective-permute-start.11) | collective-permute-done | bytes 524320 | tf_op jit(solution)/shard_map/ppermute | solution.py:23
  303.5 3.7 fusion.87
  307.2 3.4 copy.67
  310.6 3.4 copy.68
  314.5 2.9 fusion.34
  317.3 1.6 copy.79
  318.9 6.8 %collective-permute-done.12 = f32[8,32,24,4]{1,2,3,0:T(8,128)} collective-permute-done((f32[8,32,24,4]{1,2,3,0:T(8,128)}, f32[8,32,24,4]{1,2,3,0:T(8,128)}, u32[]{:S(2)}, u32[]{:S(2)}) %collective-permute-start.12) | collective-permute-done | bytes 98336 | tf_op jit(solution)/shard_map/ppermute | solution.py:21
  325.7 3.6 copy.69
  329.3 3.4 copy.70
  332.7 5.7 %pad_maximum_fusion.1 = f32[8,32,24,136]{3,1,2,0:T(8,128)S(1)} fusion(f32[8,32,24,4]{3,1,2,0:T(8,128)} %copy.70, f32[8,32,4,128]{3,1,2,0:T(8,128)S(1)} %collective-permute-done.11, f32[8,32,16,128]{3,1,2,0:T(8,128)S(1)} %copy_multiply_fusion, f32[8,32,4,128]{3,1,2,0:T(8,128)S(1)} %collective-permute-done.10, f32[8,32,24,4]{3,1,2,0:T(8,128)} %copy.69), kind=kLoop, calls=%fused_computation.17 | loop fusion | flops 3342336 | bytes 6684672 | tf_op jit(solution)/shard_map/concatenate | solution.py:19
  339.8 2.8 slice.405
  342.6 2.3 rev.25
  344.9 2.3 rev.24
  347.2 6.6 %maximum_select_fusion.2 = f32[8,32,24,136]{3,1,2,0:T(8,128)S(1)} fusion(f32[8,32,20,136]{3,1,2,0:T(8,128)} %slice.405, f32[8,32,4,136]{3,1,2,0:T(8,128)} %rev.24, pred[]{:T(512)S(6)} %eq.20, f32[8,32,24,4]{3,1,2,0:T(8,128)} %copy.70, f32[8,32,4,128]{3,1,2,0:T(8,128)S(1)} %collective-permute-done.11, f32[8,32,16,128]{3,1,2,0:T(8,128)S(1)} %copy_multiply_fusion, ...), kind=kLoop, calls=%fused_computation.18 | loop fusion | flops 5013504 | bytes 10027009 | tf_op jit(solution)/shard_map/jit(_where)/select_n | solution.py:50
  355.1 3.6 broadcast_multiply_fusion
  358.7 12.1 %broadcast_multiply_fusion.1 = (f32[8,32,22,134]{3,1,2,0:T(8,128)}, f32[8,32,22,134]{3,1,2,0:T(8,128)}) fusion(f32[22,134]{1,0:T(8,128)S(1)} %slice_bitcast_fusion.2, f32[8,32,24,136]{3,1,2,0:T(8,128)S(1)} %get-tuple-element.15, f32[8,32,24,136]{3,1,2,0:T(8,128)} %get-tuple-element.16), kind=kLoop, calls=%fused_computation.59 | loop fusion | flops 5282816 | bytes 24161808 | tf_op jit(solution)/shard_map/mul | solution.py:76
  370.7 14.0 %broadcast_multiply_fusion.2 = (f32[8,32,20,132]{3,1,2,0:T(8,128)S(1)}, f32[8,32,20,132]{3,1,2,0:T(8,128)S(1)}) fusion(f32[20,132]{1,0:T(8,128)S(1)} %slice_bitcast_fusion.1, f32[8,32,22,134]{3,1,2,0:T(8,128)} %get-tuple-element.13, f32[8,32,22,134]{3,1,2,0:T(8,128)} %get-tuple-element.14), kind=kLoop, calls=%fused_computation.60 | loop fusion | flops 4730880 | bytes 21637440 | tf_op jit(solution)/shard_map/mul | solution.py:76
  384.8 7.6 %broadcast_multiply_fusion.3 = (f32[8,32,18,130]{3,1,2,0:T(8,128)S(1)}, f32[8,32,18,130]{3,1,2,0:T(8,128)}) fusion(f32[18,130]{1,0:T(8,128)S(1)} %slice_bitcast_fusion, f32[8,32,20,132]{3,1,2,0:T(8,128)S(1)} %get-tuple-element.11, f32[8,32,20,132]{3,1,2,0:T(8,128)S(1)} %get-tuple-element.12), kind=kLoop, calls=%fused_computation.61 | loop fusion | flops 4193280 | bytes 19178640 | tf_op jit(solution)/shard_map/mul | solution.py:76
  392.5 6.8 %bitcast_add_fusion = f32[8,32,16,128]{3,1,2,0:T(8,128)S(1)} fusion(f32[8,32,16,128]{3,2,1,0:T(8,128)S(1)} %copy-done.4, f32[8,32,18,130]{3,1,2,0:T(8,128)S(1)} %get-tuple-element.9, f32[8,32,18,130]{3,1,2,0:T(8,128)} %get-tuple-element.10, s32[32]{0:T(128)S(1)} %copy-done.17, s32[32]{0:T(128)S(1)} %copy-done.15), kind=kOutput, calls=%fused_computation.77 | convolution fusion | flops 205005824 | bytes 16778240 | tf_op jit(solution)/shard_map/lm,klyx->kmyx/dot_general | solution.py:183
  399.3 2.5 copy.78
  (117 shorter events, 25.9 us)
Async XLA Ops:
  7.2 161.2 %copy-start = (f32[4,32,32]{2,1,0:T(8,128)S(1)}, f32[4,32,32]{2,1,0:T(8,128)}, u32[]{:S(2)}) copy-start(f32[4,32,32]{2,1,0:T(8,128)} %param.21) | copy-start | bytes 49156
  7.2 16.1 %copy-start.9 = (f32[16,128]{1,0:T(8,128)S(1)}, f32[16,128]{1,0:T(8,128)}, u32[]{:S(2)}) copy-start(f32[16,128]{1,0:T(8,128)} %param.19) | copy-start | bytes 24580
  7.2 15.4 %copy-start.19 = (s32[1,2]{1,0:T(1,128)S(1)}, s32[1,2]{1,0:T(1,128)}, u32[]{:S(2)}) copy-start(s32[1,2]{1,0:T(1,128)} %param.22) | copy-start | bytes 28
  7.2 161.1 %all-reduce.3.cloned.1.call-start = ((), (), s32[]{:S(2)}) async-start(), calls=%async_computation | async-start | bytes 2097152 | tf_op jit(solution)/shard_map/psum | solution.py:165
  8.0 15.3 %collective-permute-start.4 = (f32[1,1,4,128]{3,2,1,0:T(4,128)S(1)}, f32[1,1,4,128]{3,2,1,0:T(4,128)S(1)}, u32[]{:S(2)}, u32[]{:S(2)}) collective-permute-start(f32[1,1,4,128]{3,2,1,0:T(4,128)S(1)} %get-tuple-element.47), channel_id=1, source_target_pairs={{0,4},{4,8},{8,12},{12,0},{1,5},{5,9},{9,13},{13,1},{2,6},{6,10},{... | collective-permute-start | bytes 6152 | tf_op jit(solution)/shard_map/ppermute | solution.py:21
  11.0 12.3 %collective-permute-start.5 = (f32[1,1,4,128]{3,2,1,0:T(4,128)S(1)}, f32[1,1,4,128]{3,2,1,0:T(4,128)S(1)}, u32[]{:S(2)}, u32[]{:S(2)}) collective-permute-start(f32[1,1,4,128]{3,2,1,0:T(4,128)S(1)} %get-tuple-element.48), channel_id=1, source_target_pairs={{4,0},{8,4},{12,8},{0,12},{5,1},{9,5},{13,9},{1,13},{6,2},{10,6},{... | collective-permute-start | bytes 6152 | tf_op jit(solution)/shard_map/ppermute | solution.py:23
  13.8 12.8 %copy-start.14 = (s32[32]{0:T(128)}, s32[32]{0:T(128)S(1)}, u32[]{:S(2)}) copy-start(s32[32]{0:T(128)S(1)} %get-tuple-element.61) | copy-start | bytes 388
  13.8 12.8 %copy-start.16 = (s32[32]{0:T(128)}, s32[32]{0:T(128)S(1)}, u32[]{:S(2)}) copy-start(s32[32]{0:T(128)S(1)} %get-tuple-element.62) | copy-start | bytes 388
  18.7 16.8 %collective-permute-start = (f32[8,32,4,128]{3,1,2,0:T(8,128)}, f32[8,32,4,128]{3,1,2,0:T(8,128)S(1)}, u32[]{:S(2)}, u32[]{:S(2)}) collective-permute-start(f32[8,32,4,128]{3,1,2,0:T(8,128)} %get-tuple-element.31), channel_id=1, source_target_pairs={{0,4},{4,8},{8,12},{12,0},{1,5},{5,9},{9,13},{13,1},{2,6},{6,10},{... | collective-permute-start | bytes 1572872 | tf_op jit(solution)/shard_map/ppermute | solution.py:21
  18.7 24.8 %collective-permute-start.1 = (f32[8,32,4,128]{3,1,2,0:T(8,128)}, f32[8,32,4,128]{3,1,2,0:T(8,128)S(1)}, u32[]{:S(2)}, u32[]{:S(2)}) collective-permute-start(f32[8,32,4,128]{3,1,2,0:T(8,128)} %get-tuple-element.32), channel_id=1, source_target_pairs={{4,0},{8,4},{12,8},{0,12},{5,1},{9,5},{13,9},{1,13},{6,2},{10,6},{... | collective-permute-start | bytes 1572872 | tf_op jit(solution)/shard_map/ppermute | solution.py:23
  23.4 3.1 collective-permute-start.6
  23.4 3.1 collective-permute-start.7
  54.3 15.2 %collective-permute-start.3 = (f32[8,32,24,4]{1,2,3,0:T(8,128)}, f32[8,32,24,4]{1,2,3,0:T(8,128)}, u32[]{:S(2)}, u32[]{:S(2)}) collective-permute-start(f32[8,32,24,4]{1,2,3,0:T(8,128)} %copy.53), channel_id=1, source_target_pairs={{1,0},{2,1},{3,2},{0,3},{5,4},{6,5},{7,6},{4,7},{9,8},{10,9},{11,1... | collective-permute-start | bytes 294920 | tf_op jit(solution)/shard_map/ppermute | solution.py:23
  54.4 11.8 %collective-permute-start.2 = (f32[8,32,24,4]{1,2,3,0:T(8,128)}, f32[8,32,24,4]{1,2,3,0:T(8,128)}, u32[]{:S(2)}, u32[]{:S(2)}) collective-permute-start(f32[8,32,24,4]{1,2,3,0:T(8,128)} %copy.52), channel_id=1, source_target_pairs={{0,1},{1,2},{2,3},{3,0},{4,5},{5,6},{6,7},{7,4},{8,9},{9,10},{10,1... | collective-permute-start | bytes 294920 | tf_op jit(solution)/shard_map/ppermute | solution.py:21
  94.1 2.6 copy-start.2
  96.8 2.8 copy-start.7
  124.6 2.2 copy-start.3
  126.8 2.9 copy-start.18
  126.8 3.0 copy-start.13
  126.8 41.5 %copy-start.6 = (f32[4,32,16,128]{3,2,1,0:T(8,128)S(1)}, f32[4,32,16,128]{3,2,1,0:T(8,128)}, u32[]{:S(2)}) copy-start(f32[4,32,16,128]{3,2,1,0:T(8,128)} %param.18) | copy-start | bytes 3145732
  129.0 142.1 %all-reduce.5.cloned.1.call-start = ((), (), s32[]{:S(2)}) async-start(), calls=%async_computation.1 | async-start | bytes 2097152 | tf_op jit(solution)/shard_map/psum | solution.py:176
  171.8 3.6 collective-permute-start.8
  176.2 13.2 %copy-start.8 = (bf16[1024,128]{1,0:T(8,128)(2,1)S(1)}, bf16[1024,128]{1,0:T(8,128)(2,1)}, u32[]{:S(2)}) copy-start(bf16[1024,128]{1,0:T(8,128)(2,1)} %param.25) | copy-start | bytes 786436
  176.5 14.3 %copy-start.10 = (f32[8,1024]{1,0:T(8,128)S(1)}, f32[8,1024]{1,0:T(8,128)}, u32[]{:S(2)}) copy-start(f32[8,1024]{1,0:T(8,128)} %param.27) | copy-start | bytes 98308
  176.5 14.3 %copy-start.11 = (f32[8,1024]{1,0:T(8,128)S(1)}, f32[8,1024]{1,0:T(8,128)}, u32[]{:S(2)}) copy-start(f32[8,1024]{1,0:T(8,128)} %param.26) | copy-start | bytes 98308
  176.5 14.3 %copy-start.12 = (f32[8,128]{1,0:T(8,128)S(1)}, f32[8,128]{1,0:T(8,128)}, u32[]{:S(2)}) copy-start(f32[8,128]{1,0:T(8,128)} %param.28) | copy-start | bytes 12292
  223.4 6.1 %collective-permute-start.9 = (f32[16,33,128]{2,0,1:T(8,128)S(1)}, f32[16,33,128]{2,0,1:T(8,128)S(1)}, u32[]{:S(2)}, u32[]{:S(2)}) collective-permute-start(f32[16,33,128]{2,0,1:T(8,128)S(1)} %slice.398), channel_id=1, source_target_pairs={{0,1},{1,2},{2,3},{3,0},{4,5},{5,6},{6,7},{7,4},{8,9},{9,10},{10,1... | collective-permute-start | bytes 811016 | tf_op jit(solution)/shard_map/ppermute | solution.py:33
  277.2 16.7 %collective-permute-start.10 = (f32[8,32,4,128]{3,1,2,0:T(8,128)S(1)}, f32[8,32,4,128]{3,1,2,0:T(8,128)S(1)}, u32[]{:S(2)}, u32[]{:S(2)}) collective-permute-start(f32[8,32,4,128]{3,1,2,0:T(8,128)S(1)} %get-tuple-element.29), channel_id=1, source_target_pairs={{0,4},{4,8},{8,12},{12,0},{1,5},{5,9},{9,13},{13,1},{2,6},{6,10},{... | collective-permute-start | bytes 1572872 | tf_op jit(solution)/shard_map/ppermute | solution.py:21
  278.7 24.5 %collective-permute-start.11 = (f32[8,32,4,128]{3,1,2,0:T(8,128)S(1)}, f32[8,32,4,128]{3,1,2,0:T(8,128)S(1)}, u32[]{:S(2)}, u32[]{:S(2)}) collective-permute-start(f32[8,32,4,128]{3,1,2,0:T(8,128)S(1)} %get-tuple-element.30), channel_id=1, source_target_pairs={{4,0},{8,4},{12,8},{0,12},{5,1},{9,5},{13,9},{1,13},{6,2},{10,6},{... | collective-permute-start | bytes 1572872 | tf_op jit(solution)/shard_map/ppermute | solution.py:23
  314.0 15.4 %collective-permute-start.13 = (f32[8,32,24,4]{1,2,3,0:T(8,128)}, f32[8,32,24,4]{1,2,3,0:T(8,128)}, u32[]{:S(2)}, u32[]{:S(2)}) collective-permute-start(f32[8,32,24,4]{1,2,3,0:T(8,128)} %copy.68), channel_id=1, source_target_pairs={{1,0},{2,1},{3,2},{0,3},{5,4},{6,5},{7,6},{4,7},{9,8},{10,9},{11,1... | collective-permute-start | bytes 294920 | tf_op jit(solution)/shard_map/ppermute | solution.py:23
  314.5 11.3 %collective-permute-start.12 = (f32[8,32,24,4]{1,2,3,0:T(8,128)}, f32[8,32,24,4]{1,2,3,0:T(8,128)}, u32[]{:S(2)}, u32[]{:S(2)}) collective-permute-start(f32[8,32,24,4]{1,2,3,0:T(8,128)} %copy.67), channel_id=1, source_target_pairs={{0,1},{1,2},{2,3},{3,0},{4,5},{5,6},{6,7},{7,4},{8,9},{9,10},{10,1... | collective-permute-start | bytes 294920 | tf_op jit(solution)/shard_map/ppermute | solution.py:21
  353.9 1.2 copy-start.5
  384.8 7.7 %copy-start.4 = (f32[8,32,16,128]{3,2,1,0:T(8,128)S(1)}, f32[8,32,16,128]{3,2,1,0:T(8,128)}, u32[]{:S(2)}) copy-start(f32[8,32,16,128]{3,2,1,0:T(8,128)} %param.16) | copy-start | bytes 6291460
  384.8 7.7 %copy-start.15 = (s32[32]{0:T(128)S(1)}, s32[32]{0:T(128)}, u32[]{:S(2)}) copy-start(s32[32]{0:T(128)} %copy-done.14) | copy-start | bytes 388
  384.8 7.7 %copy-start.17 = (s32[32]{0:T(128)S(1)}, s32[32]{0:T(128)}, u32[]{:S(2)}) copy-start(s32[32]{0:T(128)} %copy-done.16) | copy-start | bytes 388
  392.5 9.3 %copy-start.1 = (f32[4,32,32]{2,1,0:T(8,128)S(1)}, f32[4,32,32]{2,1,0:T(8,128)}, u32[]{:S(2)}) copy-start(f32[4,32,32]{2,1,0:T(8,128)} %param.21) | copy-start | bytes 49156
Sparse Core Ops, SparseCore 0:
  129.1 39.1 all-reduce.2
  231.7 39.3 all-reduce.4
where the time goes:
time: 414 us; the launch traced here: 409 us
  waiting for transfers between devices  142 us (34%)
  other arithmetic  126 us (30%)
  local copies, waits for them, and re-layouts  88.7 us (21%)
  starting transfers between devices  18.1 us (4%)
  matrix products  17.5 us (4%)
  between operations  16.3 us (4%)
    psum x1, waiting for transfers between devices, body(): gradient_cells = lax.psum(tile_grad, 'mem')  39.5 us
    ppermute x6, waiting for transfers between devices, padded_2(): lax.ppermute(tail, axis, [(i, (i + 1) % count) for i in range(count)])  39.3 us
    psum x1, waiting for transfers between devices, body(): member_total = lax.psum(partial_sum, 'mem')  38.5 us
    mul x4, other arithmetic, sweep_adjoint(): stencil_sum = stencil_of(kappa_pad * padded)  37.3 us
    scatter-add x4, other arithmetic, observe(): returned.at[cell_index[corner]]  27.2 us
    add x4, other arithmetic, sweep_forward(): padded = padded[:, :, 1:-1, 1:-1] + kappa_pad * stencil_sum  19.1 us
    ppermute x6, waiting for transfers between devices, padded_2(): lax.ppermute(head, axis, [((i + 1) % count, i) for i in range(count)])  17.4 us
    slice x8, local copies, waits for them, and re-layouts, padded_2(): lax.slice_in_dim(cells, cells.shape[dim] - width, cells.shape[dim], axis=...  16.1 us
  transfers between devices with their start and end apart: 16, of which 11 were waited for; matrix products, arithmetic and copies ran while one was open for 5% of the time, Pallas kernels for 0%

commit v1 on v0

--- a/solution.py
+++ b/solution.py
@@ -3,6 +3,7 @@
 import jax.numpy as jnp
 from jax import lax
 from jax.sharding import PartitionSpec as P
+from jax.lax import all_gather
 
 NDIFF = 4
 ensemble_weight = 0.8
@@ -162,7 +163,8 @@
     kappa_pad = deep_pad(kappa[None, None], NDIFF)
     spread = sweep_forward(deep_pad(spread, NDIFF), kappa_pad)
     partial_sum = jnp.sum(perturb.astype(jnp.float32) * spread[:, None], axis=0)
-    member_total = lax.psum(partial_sum, "mem")
+    block_out = all_gather(partial_sum, "mem")
+    member_total = jnp.sum(block_out, 0)
     static = jnp.einsum("vlm,vmyx->vlyx", static_vert, chi, precision=highest)
     increment = (ens_scale * member_total + static_weight * static).astype(jnp.bfloat16)
     widened = extend_east(to_cells(increment, column_width), rim_cols)

time: 414 us -> 407 us (0.983)
  waiting for transfers between devices: 142 us -> 135 us
    psum x1 -> x0, waiting for transfers between devices: 38.5 us -> none  [body(): member_total = lax.psum(partial_sum, 'mem')]
    all_gather x0 -> x1, waiting for transfers between devices: none -> 29.7 us  [body(): block_out = all_gather(partial_sum, 'mem')]
where the time goes in v1:
time: 407 us; the launch traced here: 402 us
  waiting for transfers between devices  135 us (33%)
  other arithmetic  129 us (32%)
  local copies, waits for them, and re-layouts  87.3 us (21%)
  starting transfers between devices  18.3 us (4%)
  matrix products  16.6 us (4%)
  between operations  16.5 us (4%)
    ppermute x6, waiting for transfers between devices, padded_2(): lax.ppermute(tail, axis, [(i, (i + 1) % count) for i in range(count)])  40.8 us
    psum x1, waiting for transfers between devices, body(): gradient_cells = lax.psum(tile_grad, 'mem')  39.5 us
    mul x4, other arithmetic, sweep_adjoint(): stencil_sum = stencil_of(kappa_pad * padded)  37.3 us
    all_gather x1, waiting for transfers between devices, body(): block_out = all_gather(partial_sum, 'mem')  29.7 us
    scatter-add x4, other arithmetic, observe(): returned.at[cell_index[corner]]  27 us
    add x4, other arithmetic, sweep_forward(): padded = padded[:, :, 1:-1, 1:-1] + kappa_pad * stencil_sum  19.2 us
    ppermute x6, waiting for transfers between devices, padded_2(): lax.ppermute(head, axis, [((i + 1) % count, i) for i in range(count)])  17.4 us
    slice x8, local copies, waits for them, and re-layouts, padded_2(): lax.slice_in_dim(cells, cells.shape[dim] - width, cells.shape[dim], axis=...  16.1 us
  transfers between devices with their start and end apart: 16, of which 11 were waited for; matrix products, arithmetic and copies ran while one was open for 5% of the time, Pallas kernels for 0%

profile of v1, /device:TPU:0, one launch (start us, length us, event | category | flops | bytes accessed | tf_op | source)
XLA Modules:
  0.0 402.2 jit_solution(10909949520491467498)
XLA Ops:
  7.9 3.1 collective-permute-start.4
  11.0 2.0 collective-permute-start.5
  13.8 3.9 fusion.28
  18.7 3.8 collective-permute-start.1
  22.6 1.7 collective-permute-start.7
  26.5 9.1 %collective-permute-done = f32[8,32,4,128]{3,1,2,0:T(8,128)S(1)} collective-permute-done((f32[8,32,4,128]{3,1,2,0:T(8,128)}, f32[8,32,4,128]{3,1,2,0:T(8,128)S(1)}, u32[]{:S(2)}, u32[]{:S(2)}) %collective-permute-start) | collective-permute-done | bytes 524320 | tf_op jit(solution)/shard_map/ppermute | solution.py:22
  35.5 8.0 %collective-permute-done.1 = f32[8,32,4,128]{3,1,2,0:T(8,128)S(1)} collective-permute-done((f32[8,32,4,128]{3,1,2,0:T(8,128)}, f32[8,32,4,128]{3,1,2,0:T(8,128)S(1)}, u32[]{:S(2)}, u32[]{:S(2)}) %collective-permute-start.1) | collective-permute-done | bytes 524320 | tf_op jit(solution)/shard_map/ppermute | solution.py:24
  43.9 3.7 fusion.88
  47.6 3.4 copy.81
  51.0 3.4 copy.82
  55.1 11.0 %collective-permute-done.2 = f32[8,32,24,4]{1,2,3,0:T(8,128)} collective-permute-done((f32[8,32,24,4]{1,2,3,0:T(8,128)}, f32[8,32,24,4]{1,2,3,0:T(8,128)}, u32[]{:S(2)}, u32[]{:S(2)}) %collective-permute-start.2) | collective-permute-done | bytes 98336 | tf_op jit(solution)/shard_map/ppermute | solution.py:22
  66.1 3.4 copy.83
  69.6 3.4 copy.84
  72.9 5.7 %pad_maximum_fusion = f32[8,32,24,136]{3,1,2,0:T(8,128)S(1)} fusion(f32[8,32,24,4]{3,1,2,0:T(8,128)} %copy.84, f32[8,32,4,128]{3,1,2,0:T(8,128)S(1)} %collective-permute-done.1, f32[8,32,16,128]{3,1,2,0:T(8,128)S(1)} %fusion.28, f32[8,32,4,128]{3,1,2,0:T(8,128)S(1)} %collective-permute-done, f32[8,32,24,4]{3,1,2,0:T(8,128)} %copy.83), kind=kLoop, calls=%fused_computation.14 | loop fusion | flops 3342336 | bytes 6684672 | tf_op jit(solution)/shard_map/concatenate | solution.py:20
  80.1 2.8 slice.361
  82.8 2.3 rev.21
  85.2 2.3 rev.20
  87.5 6.6 %maximum_select_fusion = f32[8,32,24,136]{3,1,2,0:T(8,128)S(1)} fusion(f32[8,32,20,136]{3,1,2,0:T(8,128)} %slice.361, f32[8,32,4,136]{3,1,2,0:T(8,128)} %rev.20, pred[]{:T(512)S(6)} %eq.20, f32[8,32,24,4]{3,1,2,0:T(8,128)} %copy.84, f32[8,32,4,128]{3,1,2,0:T(8,128)S(1)} %collective-permute-done.1, f32[8,32,16,128]{3,1,2,0:T(8,128)S(1)} %fusion.28, ...), kind=kLoop, calls=%fused_computation.15 | loop fusion | flops 5013504 | bytes 10027009 | tf_op jit(solution)/shard_map/jit(_where)/select_n | solution.py:51
  94.1 2.6 copy-done.2
  96.8 2.8 slice.362
  99.6 5.9 %maximum_select_fusion.1 = f32[8,32,24,136]{3,1,2,0:T(8,128)S(1)} fusion(f32[8,32,24,136]{3,1,2,0:T(8,128)} %copy-done.2, f32[8,32,4,136]{3,1,2,0:T(8,128)S(1)} %copy-done.7, f32[8,32,20,136]{3,1,2,0:T(8,128)} %slice.362, pred[]{:T(512)S(6)} %eq.19), kind=kLoop, calls=%fused_computation.16 | loop fusion | flops 1671168 | bytes 10027009 | tf_op jit(solution)/shard_map/jit(_where)/select_n | solution.py:53
  105.5 6.1 %fusion.6 = f32[8,32,22,134]{3,1,2,0:T(8,128)S(1)} fusion(f32[8,32,24,136]{3,1,2,0:T(8,128)S(1)} %maximum_select_fusion.1, f32[22,134]{1,0:T(8,128)S(1)} %slice_bitcast_fusion.2), kind=kLoop, calls=%fused_computation.29 | loop fusion | flops 5282816 | bytes 18124304 | tf_op jit(solution)/shard_map/add | solution.py:71
  111.6 5.8 %fusion.11 = f32[8,32,20,132]{3,1,2,0:T(8,128)S(1)} fusion(f32[8,32,22,134]{3,1,2,0:T(8,128)S(1)} %fusion.6, f32[20,132]{1,0:T(8,128)S(1)} %slice_bitcast_fusion.1), kind=kLoop, calls=%fused_computation.41 | loop fusion | flops 4730880 | bytes 16230720 | tf_op jit(solution)/shard_map/add | solution.py:71
  117.4 5.0 %fusion.16 = f32[8,32,18,130]{3,1,2,0:T(8,128)S(1)} fusion(f32[8,32,20,132]{3,1,2,0:T(8,128)S(1)} %fusion.11, f32[18,130]{1,0:T(8,128)S(1)} %slice_bitcast_fusion), kind=kLoop, calls=%fused_computation.53 | loop fusion | flops 4193280 | bytes 14386320 | tf_op jit(solution)/shard_map/add | solution.py:71
  122.5 2.2 fusion.25
  126.9 1.8 fusion
  131.3 29.7 %all-gather.3.cloned.1.call-done = f32[8,32,16,128]{3,2,1,0:T(8,128)} async-done(((f32[4,32,16,128]{3,2,1,0:T(8,128)}), f32[8,32,16,128]{3,2,1,0:T(8,128)}) %all-gather.3.cloned.1.call-update) | async-done | bytes 2097168 | tf_op jit(solution)/shard_map/all_gather | solution.py:166
  161.1 1.9 reduce_sum.38
  166.4 2.4 collective-permute-done.8
  170.0 3.2 gather_fusion.4
  173.2 3.2 gather_fusion.3
  176.5 3.2 gather_fusion.2
  179.7 3.2 gather_fusion.1
  185.9 6.7 %scatter_custom_fusion = f32[1040,128]{1,0:T(8,128)S(1)} fusion(s32[1024]{0:T(1024)S(1)} %get-tuple-element.66, f32[1024,128]{1,0:T(8,128)S(1)} %convolution_multiply_fusion.2, f32[]{:T(128)} %constant.45.clone.1, f32[1024]{0:T(1024)S(1)} %bitcast.98), kind=kCustom, calls=%fused_computation.104 | custom fusion | flops 262144 | bytes 1060868 | tf_op jit(solution)/shard_map/scatter-add | solution.py:126
  192.5 6.7 %scatter_custom_fusion.1 = f32[1040,128]{1,0:T(8,128)S(1)} fusion(f32[1040,128]{1,0:T(8,128)S(1)} %scatter_custom_fusion, s32[1024]{0:T(1024)S(1)} %get-tuple-element.61, f32[1024,128]{1,0:T(8,128)S(1)} %convolution_multiply_fusion.2, f32[1024]{0:T(1024)S(1)} %bitcast.96), kind=kCustom, calls=%fused_computation.102 | custom fusion | flops 262144 | bytes 1060864 | tf_op jit(solution)/shard_map/scatter-add | solution.py:126
  199.2 6.9 %scatter_custom_fusion.2 = f32[1040,128]{1,0:T(8,128)S(1)} fusion(f32[1040,128]{1,0:T(8,128)S(1)} %scatter_custom_fusion.1, s32[1024]{0:T(1024)S(1)} %get-tuple-element.51, f32[1024,128]{1,0:T(8,128)S(1)} %convolution_multiply_fusion.2, f32[1024]{0:T(1024)S(1)} %bitcast.94), kind=kCustom, calls=%fused_computation.100 | custom fusion | flops 262144 | bytes 1060864 | tf_op jit(solution)/shard_map/scatter-add | solution.py:126
  206.1 6.7 %scatter_custom_fusion.3 = f32[1040,128]{1,0:T(8,128)S(1)} fusion(f32[1040,128]{1,0:T(8,128)S(1)} %scatter_custom_fusion.2, s32[1024]{0:T(1024)S(1)} %get-tuple-element.19, f32[1024,128]{1,0:T(8,128)S(1)} %convolution_multiply_fusion.2, f32[1024]{0:T(1024)S(1)} %bitcast.92), kind=kCustom, calls=%fused_computation.98 | custom fusion | flops 262144 | bytes 1060864 | tf_op jit(solution)/shard_map/scatter-add | solution.py:126
  213.1 3.5 scatter_fusion
  217.7 5.0 %collective-permute-done.9 = f32[16,33,128]{2,0,1:T(8,128)S(1)} collective-permute-done((f32[16,33,128]{2,0,1:T(8,128)S(1)}, f32[16,33,128]{2,0,1:T(8,128)S(1)}, u32[]{:S(2)}, u32[]{:S(2)}) %collective-permute-start.9) | collective-permute-done | bytes 270368 | tf_op jit(solution)/shard_map/ppermute | solution.py:34
  224.8 39.5 %all-reduce.2.cloned.1.call-done = f32[4,32,16,128]{3,1,2,0:T(8,128)} async-done(((f32[4,32,16,128]{3,1,2,0:T(8,128)}), f32[4,32,16,128]{3,1,2,0:T(8,128)}) %all-reduce.2.cloned.1.call-update) | async-done | bytes 1048592 | tf_op jit(solution)/shard_map/psum | solution.py:178
  264.3 1.8 copy.94
  266.2 3.4 fusion.1
  272.0 2.3 collective-permute-start.11
  274.4 12.7 %collective-permute-done.10 = f32[8,32,4,128]{3,1,2,0:T(8,128)S(1)} collective-permute-done((f32[8,32,4,128]{3,1,2,0:T(8,128)S(1)}, f32[8,32,4,128]{3,1,2,0:T(8,128)S(1)}, u32[]{:S(2)}, u32[]{:S(2)}) %collective-permute-start.10) | collective-permute-done | bytes 524320 | tf_op jit(solution)/shard_map/ppermute | solution.py:22
  287.1 9.3 %collective-permute-done.11 = f32[8,32,4,128]{3,1,2,0:T(8,128)S(1)} collective-permute-done((f32[8,32,4,128]{3,1,2,0:T(8,128)S(1)}, f32[8,32,4,128]{3,1,2,0:T(8,128)S(1)}, u32[]{:S(2)}, u32[]{:S(2)}) %collective-permute-start.11) | collective-permute-done | bytes 524320 | tf_op jit(solution)/shard_map/ppermute | solution.py:24
  296.8 3.7 fusion.87
  300.5 3.4 copy.96
  303.8 3.4 copy.97
  307.9 2.9 fusion.34
  310.8 1.6 copy.108
  312.4 6.6 %collective-permute-done.12 = f32[8,32,24,4]{1,2,3,0:T(8,128)} collective-permute-done((f32[8,32,24,4]{1,2,3,0:T(8,128)}, f32[8,32,24,4]{1,2,3,0:T(8,128)}, u32[]{:S(2)}, u32[]{:S(2)}) %collective-permute-start.12) | collective-permute-done | bytes 98336 | tf_op jit(solution)/shard_map/ppermute | solution.py:22
  319.0 3.4 copy.98
  322.4 3.4 copy.99
  325.8 5.7 %pad_maximum_fusion.1 = f32[8,32,24,136]{3,1,2,0:T(8,128)S(1)} fusion(f32[8,32,24,4]{3,1,2,0:T(8,128)} %copy.99, f32[8,32,4,128]{3,1,2,0:T(8,128)S(1)} %collective-permute-done.11, f32[8,32,16,128]{3,1,2,0:T(8,128)S(1)} %copy_multiply_fusion, f32[8,32,4,128]{3,1,2,0:T(8,128)S(1)} %collective-permute-done.10, f32[8,32,24,4]{3,1,2,0:T(8,128)} %copy.98), kind=kLoop, calls=%fused_computation.17 | loop fusion | flops 3342336 | bytes 6684672 | tf_op jit(solution)/shard_map/concatenate | solution.py:20
  333.0 2.8 slice.405
  335.7 2.3 rev.25
  338.1 2.3 rev.24
  340.4 6.6 %maximum_select_fusion.2 = f32[8,32,24,136]{3,1,2,0:T(8,128)S(1)} fusion(f32[8,32,20,136]{3,1,2,0:T(8,128)} %slice.405, f32[8,32,4,136]{3,1,2,0:T(8,128)} %rev.24, pred[]{:T(512)S(6)} %eq.20, f32[8,32,24,4]{3,1,2,0:T(8,128)} %copy.99, f32[8,32,4,128]{3,1,2,0:T(8,128)S(1)} %collective-permute-done.11, f32[8,32,16,128]{3,1,2,0:T(8,128)S(1)} %copy_multiply_fusion, ...), kind=kLoop, calls=%fused_computation.18 | loop fusion | flops 5013504 | bytes 10027009 | tf_op jit(solution)/shard_map/jit(_where)/select_n | solution.py:51
  348.2 3.6 broadcast_multiply_fusion
  351.8 12.1 %broadcast_multiply_fusion.1 = (f32[8,32,22,134]{3,1,2,0:T(8,128)}, f32[8,32,22,134]{3,1,2,0:T(8,128)}) fusion(f32[22,134]{1,0:T(8,128)S(1)} %slice_bitcast_fusion.2, f32[8,32,24,136]{3,1,2,0:T(8,128)S(1)} %get-tuple-element.17, f32[8,32,24,136]{3,1,2,0:T(8,128)} %get-tuple-element.18), kind=kLoop, calls=%fused_computation.59 | loop fusion | flops 5282816 | bytes 24161808 | tf_op jit(solution)/shard_map/mul | solution.py:77
  363.9 14.1 %broadcast_multiply_fusion.2 = (f32[8,32,20,132]{3,1,2,0:T(8,128)S(1)}, f32[8,32,20,132]{3,1,2,0:T(8,128)S(1)}) fusion(f32[20,132]{1,0:T(8,128)S(1)} %slice_bitcast_fusion.1, f32[8,32,22,134]{3,1,2,0:T(8,128)} %get-tuple-element.15, f32[8,32,22,134]{3,1,2,0:T(8,128)} %get-tuple-element.16), kind=kLoop, calls=%fused_computation.60 | loop fusion | flops 4730880 | bytes 21637440 | tf_op jit(solution)/shard_map/mul | solution.py:77
  378.0 7.6 %broadcast_multiply_fusion.3 = (f32[8,32,18,130]{3,1,2,0:T(8,128)S(1)}, f32[8,32,18,130]{3,1,2,0:T(8,128)}) fusion(f32[18,130]{1,0:T(8,128)S(1)} %slice_bitcast_fusion, f32[8,32,20,132]{3,1,2,0:T(8,128)S(1)} %get-tuple-element.13, f32[8,32,20,132]{3,1,2,0:T(8,128)S(1)} %get-tuple-element.14), kind=kLoop, calls=%fused_computation.61 | loop fusion | flops 4193280 | bytes 19178640 | tf_op jit(solution)/shard_map/mul | solution.py:77
  385.6 6.8 %bitcast_add_fusion = f32[8,32,16,128]{3,1,2,0:T(8,128)S(1)} fusion(f32[8,32,16,128]{3,2,1,0:T(8,128)S(1)} %copy-done.4, f32[8,32,18,130]{3,1,2,0:T(8,128)S(1)} %get-tuple-element.11, f32[8,32,18,130]{3,1,2,0:T(8,128)} %get-tuple-element.12, s32[32]{0:T(128)S(1)} %copy-done.17, s32[32]{0:T(128)S(1)} %copy-done.15), kind=kOutput, calls=%fused_computation.77 | convolution fusion | flops 205005824 | bytes 16778240 | tf_op jit(solution)/shard_map/lm,klyx->kmyx/dot_general | solution.py:185
  392.4 2.5 copy.107
  (117 shorter events, 27.7 us)
Async XLA Ops:
  7.2 155.8 %copy-start = (f32[4,32,32]{2,1,0:T(8,128)S(1)}, f32[4,32,32]{2,1,0:T(8,128)}, u32[]{:S(2)}) copy-start(f32[4,32,32]{2,1,0:T(8,128)} %param.21) | copy-start | bytes 49156
  7.2 15.4 %copy-start.9 = (f32[16,128]{1,0:T(8,128)S(1)}, f32[16,128]{1,0:T(8,128)}, u32[]{:S(2)}) copy-start(f32[16,128]{1,0:T(8,128)} %param.19) | copy-start | bytes 24580
  7.2 153.9 %all-gather.3.cloned.1.call-start = ((), (), s32[]{:S(2)}) async-start(), calls=%async_computation.1 | async-start | bytes 3145728 | tf_op jit(solution)/shard_map/all_gather | solution.py:166
  7.9 14.6 %collective-permute-start.4 = (f32[1,1,4,128]{3,2,1,0:T(4,128)S(1)}, f32[1,1,4,128]{3,2,1,0:T(4,128)S(1)}, u32[]{:S(2)}, u32[]{:S(2)}) collective-permute-start(f32[1,1,4,128]{3,2,1,0:T(4,128)S(1)} %get-tuple-element.49), channel_id=1, source_target_pairs={{0,4},{4,8},{8,12},{12,0},{1,5},{5,9},{9,13},{13,1},{2,6},{6,10},{... | collective-permute-start | bytes 6152 | tf_op jit(solution)/shard_map/ppermute | solution.py:22
  11.0 11.5 %collective-permute-start.5 = (f32[1,1,4,128]{3,2,1,0:T(4,128)S(1)}, f32[1,1,4,128]{3,2,1,0:T(4,128)S(1)}, u32[]{:S(2)}, u32[]{:S(2)}) collective-permute-start(f32[1,1,4,128]{3,2,1,0:T(4,128)S(1)} %get-tuple-element.50), channel_id=1, source_target_pairs={{4,0},{8,4},{12,8},{0,12},{5,1},{9,5},{13,9},{1,13},{6,2},{10,6},{... | collective-permute-start | bytes 6152 | tf_op jit(solution)/shard_map/ppermute | solution.py:24
  13.8 12.1 %copy-start.14 = (s32[32]{0:T(128)}, s32[32]{0:T(128)S(1)}, u32[]{:S(2)}) copy-start(s32[32]{0:T(128)S(1)} %get-tuple-element.63) | copy-start | bytes 388
  13.8 12.1 %copy-start.16 = (s32[32]{0:T(128)}, s32[32]{0:T(128)S(1)}, u32[]{:S(2)}) copy-start(s32[32]{0:T(128)S(1)} %get-tuple-element.64) | copy-start | bytes 388
  18.7 16.8 %collective-permute-start = (f32[8,32,4,128]{3,1,2,0:T(8,128)}, f32[8,32,4,128]{3,1,2,0:T(8,128)S(1)}, u32[]{:S(2)}, u32[]{:S(2)}) collective-permute-start(f32[8,32,4,128]{3,1,2,0:T(8,128)} %get-tuple-element.33), channel_id=1, source_target_pairs={{0,4},{4,8},{8,12},{12,0},{1,5},{5,9},{9,13},{13,1},{2,6},{6,10},{... | collective-permute-start | bytes 1572872 | tf_op jit(solution)/shard_map/ppermute | solution.py:22
  18.7 24.8 %collective-permute-start.1 = (f32[8,32,4,128]{3,1,2,0:T(8,128)}, f32[8,32,4,128]{3,1,2,0:T(8,128)S(1)}, u32[]{:S(2)}, u32[]{:S(2)}) collective-permute-start(f32[8,32,4,128]{3,1,2,0:T(8,128)} %get-tuple-element.34), channel_id=1, source_target_pairs={{4,0},{8,4},{12,8},{0,12},{5,1},{9,5},{13,9},{1,13},{6,2},{10,6},{... | collective-permute-start | bytes 1572872 | tf_op jit(solution)/shard_map/ppermute | solution.py:24
  22.6 3.1 collective-permute-start.6
  22.6 3.1 collective-permute-start.7
  54.3 15.2 %collective-permute-start.3 = (f32[8,32,24,4]{1,2,3,0:T(8,128)}, f32[8,32,24,4]{1,2,3,0:T(8,128)}, u32[]{:S(2)}, u32[]{:S(2)}) collective-permute-start(f32[8,32,24,4]{1,2,3,0:T(8,128)} %copy.82), channel_id=1, source_target_pairs={{1,0},{2,1},{3,2},{0,3},{5,4},{6,5},{7,6},{4,7},{9,8},{10,9},{11,1... | collective-permute-start | bytes 294920 | tf_op jit(solution)/shard_map/ppermute | solution.py:24
  54.3 11.8 %collective-permute-start.2 = (f32[8,32,24,4]{1,2,3,0:T(8,128)}, f32[8,32,24,4]{1,2,3,0:T(8,128)}, u32[]{:S(2)}, u32[]{:S(2)}) collective-permute-start(f32[8,32,24,4]{1,2,3,0:T(8,128)} %copy.81), channel_id=1, source_target_pairs={{0,1},{1,2},{2,3},{3,0},{4,5},{5,6},{6,7},{7,4},{8,9},{9,10},{10,1... | collective-permute-start | bytes 294920 | tf_op jit(solution)/shard_map/ppermute | solution.py:22
  94.1 2.6 copy-start.2
  96.8 2.8 copy-start.7
  124.7 2.2 copy-start.3
  126.9 3.0 copy-start.19
  126.9 4.4 %copy-start.18 = (s32[1024]{0:T(1024)S(1)}, s32[1024]{0:T(1024)}, u32[]{:S(2)}) copy-start(s32[1024]{0:T(1024)} %param.23) | copy-start | bytes 12292
  126.9 4.4 %copy-start.13 = (f32[4,1024]{1,0:T(4,128)S(1)}, f32[4,1024]{1,0:T(4,128)}, u32[]{:S(2)}) copy-start(f32[4,1024]{1,0:T(4,128)} %param.24) | copy-start | bytes 49156
  126.9 36.1 %copy-start.6 = (f32[4,32,16,128]{3,2,1,0:T(8,128)S(1)}, f32[4,32,16,128]{3,2,1,0:T(8,128)}, u32[]{:S(2)}) copy-start(f32[4,32,16,128]{3,2,1,0:T(8,128)} %param.18) | copy-start | bytes 3145732
  128.7 135.6 %all-reduce.2.cloned.1.call-start = ((), (), s32[]{:S(2)}) async-start(), calls=%async_computation | async-start | bytes 2097152 | tf_op jit(solution)/shard_map/psum | solution.py:178
  165.5 3.4 collective-permute-start.8
  169.7 13.2 %copy-start.8 = (bf16[1024,128]{1,0:T(8,128)(2,1)S(1)}, bf16[1024,128]{1,0:T(8,128)(2,1)}, u32[]{:S(2)}) copy-start(bf16[1024,128]{1,0:T(8,128)(2,1)} %param.25) | copy-start | bytes 786436
  170.0 14.3 %copy-start.10 = (f32[8,1024]{1,0:T(8,128)S(1)}, f32[8,1024]{1,0:T(8,128)}, u32[]{:S(2)}) copy-start(f32[8,1024]{1,0:T(8,128)} %param.27) | copy-start | bytes 98308
  170.0 14.3 %copy-start.11 = (f32[8,1024]{1,0:T(8,128)S(1)}, f32[8,1024]{1,0:T(8,128)}, u32[]{:S(2)}) copy-start(f32[8,1024]{1,0:T(8,128)} %param.26) | copy-start | bytes 98308
  170.0 14.3 %copy-start.12 = (f32[8,128]{1,0:T(8,128)S(1)}, f32[8,128]{1,0:T(8,128)}, u32[]{:S(2)}) copy-start(f32[8,128]{1,0:T(8,128)} %param.28) | copy-start | bytes 12292
  216.6 6.1 %collective-permute-start.9 = (f32[16,33,128]{2,0,1:T(8,128)S(1)}, f32[16,33,128]{2,0,1:T(8,128)S(1)}, u32[]{:S(2)}, u32[]{:S(2)}) collective-permute-start(f32[16,33,128]{2,0,1:T(8,128)S(1)} %slice.398), channel_id=1, source_target_pairs={{0,1},{1,2},{2,3},{3,0},{4,5},{5,6},{6,7},{7,4},{8,9},{9,10},{10,1... | collective-permute-start | bytes 811016 | tf_op jit(solution)/shard_map/ppermute | solution.py:34
  270.5 16.7 %collective-permute-start.10 = (f32[8,32,4,128]{3,1,2,0:T(8,128)S(1)}, f32[8,32,4,128]{3,1,2,0:T(8,128)S(1)}, u32[]{:S(2)}, u32[]{:S(2)}) collective-permute-start(f32[8,32,4,128]{3,1,2,0:T(8,128)S(1)} %get-tuple-element.31), channel_id=1, source_target_pairs={{0,4},{4,8},{8,12},{12,0},{1,5},{5,9},{9,13},{13,1},{2,6},{6,10},{... | collective-permute-start | bytes 1572872 | tf_op jit(solution)/shard_map/ppermute | solution.py:22
  272.0 24.5 %collective-permute-start.11 = (f32[8,32,4,128]{3,1,2,0:T(8,128)S(1)}, f32[8,32,4,128]{3,1,2,0:T(8,128)S(1)}, u32[]{:S(2)}, u32[]{:S(2)}) collective-permute-start(f32[8,32,4,128]{3,1,2,0:T(8,128)S(1)} %get-tuple-element.32), channel_id=1, source_target_pairs={{4,0},{8,4},{12,8},{0,12},{5,1},{9,5},{13,9},{1,13},{6,2},{10,6},{... | collective-permute-start | bytes 1572872 | tf_op jit(solution)/shard_map/ppermute | solution.py:24
  307.2 15.2 %collective-permute-start.13 = (f32[8,32,24,4]{1,2,3,0:T(8,128)}, f32[8,32,24,4]{1,2,3,0:T(8,128)}, u32[]{:S(2)}, u32[]{:S(2)}) collective-permute-start(f32[8,32,24,4]{1,2,3,0:T(8,128)} %copy.97), channel_id=1, source_target_pairs={{1,0},{2,1},{3,2},{0,3},{5,4},{6,5},{7,6},{4,7},{9,8},{10,9},{11,1... | collective-permute-start | bytes 294920 | tf_op jit(solution)/shard_map/ppermute | solution.py:24
  307.7 11.3 %collective-permute-start.12 = (f32[8,32,24,4]{1,2,3,0:T(8,128)}, f32[8,32,24,4]{1,2,3,0:T(8,128)}, u32[]{:S(2)}, u32[]{:S(2)}) collective-permute-start(f32[8,32,24,4]{1,2,3,0:T(8,128)} %copy.96), channel_id=1, source_target_pairs={{0,1},{1,2},{2,3},{3,0},{4,5},{5,6},{6,7},{7,4},{8,9},{9,10},{10,1... | collective-permute-start | bytes 294920 | tf_op jit(solution)/shard_map/ppermute | solution.py:22
  347.0 1.2 copy-start.5
  378.0 7.7 %copy-start.4 = (f32[8,32,16,128]{3,2,1,0:T(8,128)S(1)}, f32[8,32,16,128]{3,2,1,0:T(8,128)}, u32[]{:S(2)}) copy-start(f32[8,32,16,128]{3,2,1,0:T(8,128)} %param.16) | copy-start | bytes 6291460
  378.0 7.7 %copy-start.15 = (s32[32]{0:T(128)S(1)}, s32[32]{0:T(128)}, u32[]{:S(2)}) copy-start(s32[32]{0:T(128)} %copy-done.14) | copy-start | bytes 388
  378.0 7.7 %copy-start.17 = (s32[32]{0:T(128)S(1)}, s32[32]{0:T(128)}, u32[]{:S(2)}) copy-start(s32[32]{0:T(128)} %copy-done.16) | copy-start | bytes 388
  385.6 9.3 %copy-start.1 = (f32[4,32,32]{2,1,0:T(8,128)S(1)}, f32[4,32,32]{2,1,0:T(8,128)}, u32[]{:S(2)}) copy-start(f32[4,32,32]{2,1,0:T(8,128)} %param.21) | copy-start | bytes 49156
Sparse Core Ops, SparseCore 0:
  128.8 32.1 all-gather.2
  225.0 39.3 all-reduce.1
